TPU v7x, 32 devices: a whole 2x2x4 slice. The times are simulated.
32 devices in a mesh: cell: 2 (over core), gene: 4 (over y, x), rank: 4 (over z).
Axes of the slice: x: 2, y: 2, z: 4, core: 2. Of those that a mesh axis runs over, the one named last changes fastest.
Arguments:
- blocks: bfloat16 [2, 16, 96, 256, 128], P('cell', ('gene', 'rank')), may hold values from -6 to 6
- block_pos: int32 [2, 16, 96], P('cell', ('gene', 'rank')), may hold values from 0 to 127, as said below
- block_count: int32 [2, 16], P('cell', ('gene', 'rank')), may hold values from 32 to 96, as said below
- test_right: bfloat16 [32768, 512], P(('gene', 'rank')), may hold values from -0.0625 to 0.0625
- test_left: bfloat16 [4096, 768], P('cell', 'rank'), may hold values from -0.1875 to 0.1875
- gene_sketch_old: float32 [768, 32768], P('cell', ('gene', 'rank')), may hold values from -4 to 4
Outputs:
- right_sketch: float32 [4096, 512], P(('cell', 'gene', 'rank'))
- gene_sketch: float32 [768, 32768], P('cell', ('gene', 'rank'))
- core: float32 [768, 512], P('cell')
Inputs may be any that keep to these rules, and one draw needn't show every extreme that they name: `block_pos`: position p names row block p // 16 and gene block p % 16 of the device's tile; the 96 positions of one device are distinct. `block_count`: some device has all 96 slots live in every draw; slots from the count on are not part of A.
All inputs are finite; a program needn't handle non-finite values.
Results may differ from a plain program's by a relative error of at most 0.0003.
Values may be sent and summed in bfloat16 or wider, within the bound.
A program may use at most 128 MiB of HBM per device.

v0:
```python
import jax
import jax.numpy as jnp
from jax import lax
from jax.sharding import PartitionSpec as P

GROUP = 16


def body(blocks, block_pos, block_count, test_right, test_left, gene_sketch_old):
    highest = lax.Precision.HIGHEST
    tiles = blocks[0, 0]
    positions = block_pos[0, 0]
    live_count = block_count[0, 0]
    slots, block_rows, block_cols = tiles.shape
    gene_blocks = test_right.shape[0] // block_cols
    right_width = test_right.shape[1]
    left_full = lax.all_gather(test_left, "rank", axis=1, tiled=True)
    row_blocks = left_full.shape[0] // block_rows
    left_width = left_full.shape[1]
    right_table = test_right.reshape(gene_blocks, block_cols, right_width)
    left_table = left_full.reshape(row_blocks, block_rows, left_width)
    offsets = jnp.arange(GROUP, dtype=jnp.int32)

    def visit(turn_index, carry):
        right_acc, gene_acc = carry
        first_slot = turn_index * GROUP
        group_tiles = lax.dynamic_slice_in_dim(tiles, first_slot, GROUP, 0)
        group_places = lax.dynamic_slice_in_dim(positions, first_slot, GROUP, 0)
        alive_mask = (first_slot + offsets < live_count).astype(jnp.float32)
        row_block = group_places // gene_blocks
        gene_block = group_places % gene_blocks
        right_rows = jnp.take(right_table, gene_block, axis=0)
        left_rows = jnp.take(left_table, row_block, axis=0)
        right_terms = (
            jnp.einsum("pik,pkr->pir", group_tiles, right_rows, preferred_element_type=jnp.float32)
            * alive_mask[:, None, None]
        )
        gene_terms = (
            jnp.einsum("pil,pik->lpk", left_rows, group_tiles, preferred_element_type=jnp.float32)
            * alive_mask[None, :, None]
        )
        right_acc = right_acc.at[row_block].add(right_terms)
        gene_acc = gene_acc.at[:, gene_block].add(gene_terms)
        return (right_acc, gene_acc)

    turn_count = (live_count + GROUP - 1) // GROUP
    initial = (
        jnp.zeros((row_blocks, block_rows, right_width), jnp.float32),
        jnp.zeros((left_width, gene_blocks, block_cols), jnp.float32),
    )
    right_part, gene_part = lax.fori_loop(0, turn_count, visit, initial)
    right_flat = right_part.reshape(row_blocks * block_rows, right_width)
    gene_flat = gene_part.reshape(left_width, gene_blocks * block_cols)
    right_half = lax.psum_scatter(right_flat, "gene", scatter_dimension=0, tiled=True)
    right_mine = lax.psum_scatter(right_half, "rank", scatter_dimension=0, tiled=True)
    gene_mine = lax.psum_scatter(gene_flat, "cell", scatter_dimension=0, tiled=True)
    gene_sketch = gene_sketch_old + gene_mine
    shard_index = lax.axis_index("gene") * lax.axis_size("rank") + lax.axis_index("rank")
    mine_rows = right_mine.shape[0]
    left_mine = lax.dynamic_slice_in_dim(left_full, shard_index * mine_rows, mine_rows, 0).astype(
        jnp.float32
    )
    core_part = lax.dot_general(left_mine, right_mine, (((0,), (0,)), ((), ())), precision=highest)
    core_total = lax.psum(core_part, ("cell", "gene", "rank"))
    share = left_width // lax.axis_size("cell")
    core = lax.dynamic_slice_in_dim(core_total, lax.axis_index("cell") * share, share, 0)
    return (right_mine, gene_sketch, core)


def solution(mesh):
    return jax.shard_map(
        body,
        mesh=mesh,
        in_specs=(
            P("cell", ("gene", "rank"), None, None, None),
            P("cell", ("gene", "rank"), None),
            P("cell", ("gene", "rank")),
            P(("gene", "rank"), None),
            P("cell", "rank"),
            P("cell", ("gene", "rank")),
        ),
        out_specs=(P(("cell", "gene", "rank"), None), P("cell", ("gene", "rank")), P("cell", None)),
        check_vma=False,
    )
```

profile of v0, /device:TPU:1, one launch (start us, length us, event | category | flops | bytes accessed | tf_op | source)
XLA Modules:
  0.0 695.8 jit_solution(15199658908383752672)
XLA Ops:
  8.6 66.3 %all-gather.2.cloned.1.call-done = bf16[2048,768]{0,1:T(8,128)(2,1)} async-done(((bf16[2048,192]{0,1:T(8,128)(2,1)}), bf16[2048,768]{0,1:T(8,128)(2,1)}) %all-gather.2.cloned.1.call-update) | async-done | bytes 3145744 | tf_op jit(solution)/shard_map/all_gather | solution.py:17
  84.0 305.6 %while.15 = (s32[]{:T(128)}, f32[8,256,512]{2,1,0:T(8,128)}, f32[768,16,128]{2,0,1:T(8,128)}, s32[]{:T(128)}, s32[96]{0:T(128)S(1)}, /*index=5*/bf16[96,256,128]...) while((s32[]{:T(128)}, f32[8,256,512]{2,1,0:T(8,128)}, ...), condition=%wide.region_3.4_spmd.clone, body=%wide.region_0.3_spmd.clone.sunk | while | flops 1353714176 | bytes 98575488 | solution.py:51
  88.3 7.2 %multiply_bitcast_fusion.2 = f32[16,768,128]{1,2,0:T(8,128)} fusion(f32[16]{0:T(128)S(1)} %get-tuple-element.245, bf16[16,256,768]{2,1,0:T(8,128)(2,1)} %gather_fusion.1, pred[16]{0:T(512)(128)(4,1)S(1)} %get-tuple-element.249, bf16[96,256,128]{2,1,0:T(8,128)(2,1)} %get-tuple-element.281, s32[]{:T(128)S(6)} %select_n.101), kind=kOutput, calls=%fused_computation.5.clone.1 | convolution fusion | flops 810024960 | bytes 13631572 | tf_op jit(solution)/shard_map/while/body/pil,pik->lpk/dot_general | solution.py:39
  95.5 6.5 copy.17
  102.0 15.0 %scatter_fusion.1 = f32[768,16,128]{2,0,1:T(8,128)} fusion(f32[768,16,128]{2,0,1:T(8,128)} %get-tuple-element.265, s32[16]{0:T(128)S(1)} %get-tuple-element.247, f32[16,768,128]{2,1,0:T(8,128)} %copy.17), kind=kCustom, calls=%fused_computation.3.clone.clone.1 | custom fusion | flops 1572864 | bytes 18874432 | tf_op jit(solution)/shard_map/while/body/scatter-add | solution.py:43
  120.6 6.5 broadcast_multiply_fusion.2
  127.1 18.1 %scatter_fusion = f32[8,256,512]{2,1,0:T(8,128)} fusion(f32[8,256,512]{2,1,0:T(8,128)} %get-tuple-element.264, s32[16]{0:T(128)S(1)} %get-tuple-element.244, f32[16,256,512]{2,1,0:T(8,128)} %broadcast_multiply_fusion.2), kind=kCustom, calls=%fused_computation.2.clone.clone.1 | custom fusion | flops 2097152 | bytes 25165888 | tf_op jit(solution)/shard_map/while/body/scatter-add | solution.py:42
  149.4 7.2 %multiply_bitcast_fusion.2 = f32[16,768,128]{1,2,0:T(8,128)} fusion(f32[16]{0:T(128)S(1)} %get-tuple-element.245, bf16[16,256,768]{2,1,0:T(8,128)(2,1)} %gather_fusion.1, pred[16]{0:T(512)(128)(4,1)S(1)} %get-tuple-element.249, bf16[96,256,128]{2,1,0:T(8,128)(2,1)} %get-tuple-element.281, s32[]{:T(128)S(6)} %select_n.101), kind=kOutput, calls=%fused_computation.5.clone.1 | convolution fusion | flops 810024960 | bytes 13631572 | tf_op jit(solution)/shard_map/while/body/pil,pik->lpk/dot_general | solution.py:39
  156.6 6.5 copy.17
  163.2 15.3 %scatter_fusion.1 = f32[768,16,128]{2,0,1:T(8,128)} fusion(f32[768,16,128]{2,0,1:T(8,128)} %get-tuple-element.265, s32[16]{0:T(128)S(1)} %get-tuple-element.247, f32[16,768,128]{2,1,0:T(8,128)} %copy.17), kind=kCustom, calls=%fused_computation.3.clone.clone.1 | custom fusion | flops 1572864 | bytes 18874432 | tf_op jit(solution)/shard_map/while/body/scatter-add | solution.py:43
  182.1 6.5 broadcast_multiply_fusion.2
  188.5 18.0 %scatter_fusion = f32[8,256,512]{2,1,0:T(8,128)} fusion(f32[8,256,512]{2,1,0:T(8,128)} %get-tuple-element.264, s32[16]{0:T(128)S(1)} %get-tuple-element.244, f32[16,256,512]{2,1,0:T(8,128)} %broadcast_multiply_fusion.2), kind=kCustom, calls=%fused_computation.2.clone.clone.1 | custom fusion | flops 2097152 | bytes 25165888 | tf_op jit(solution)/shard_map/while/body/scatter-add | solution.py:42
  210.8 7.2 %multiply_bitcast_fusion.2 = f32[16,768,128]{1,2,0:T(8,128)} fusion(f32[16]{0:T(128)S(1)} %get-tuple-element.245, bf16[16,256,768]{2,1,0:T(8,128)(2,1)} %gather_fusion.1, pred[16]{0:T(512)(128)(4,1)S(1)} %get-tuple-element.249, bf16[96,256,128]{2,1,0:T(8,128)(2,1)} %get-tuple-element.281, s32[]{:T(128)S(6)} %select_n.101), kind=kOutput, calls=%fused_computation.5.clone.1 | convolution fusion | flops 810024960 | bytes 13631572 | tf_op jit(solution)/shard_map/while/body/pil,pik->lpk/dot_general | solution.py:39
  218.0 6.5 copy.17
  224.6 14.9 %scatter_fusion.1 = f32[768,16,128]{2,0,1:T(8,128)} fusion(f32[768,16,128]{2,0,1:T(8,128)} %get-tuple-element.265, s32[16]{0:T(128)S(1)} %get-tuple-element.247, f32[16,768,128]{2,1,0:T(8,128)} %copy.17), kind=kCustom, calls=%fused_computation.3.clone.clone.1 | custom fusion | flops 1572864 | bytes 18874432 | tf_op jit(solution)/shard_map/while/body/scatter-add | solution.py:43
  243.1 6.5 broadcast_multiply_fusion.2
  249.6 18.0 %scatter_fusion = f32[8,256,512]{2,1,0:T(8,128)} fusion(f32[8,256,512]{2,1,0:T(8,128)} %get-tuple-element.264, s32[16]{0:T(128)S(1)} %get-tuple-element.244, f32[16,256,512]{2,1,0:T(8,128)} %broadcast_multiply_fusion.2), kind=kCustom, calls=%fused_computation.2.clone.clone.1 | custom fusion | flops 2097152 | bytes 25165888 | tf_op jit(solution)/shard_map/while/body/scatter-add | solution.py:42
  271.9 7.2 %multiply_bitcast_fusion.2 = f32[16,768,128]{1,2,0:T(8,128)} fusion(f32[16]{0:T(128)S(1)} %get-tuple-element.245, bf16[16,256,768]{2,1,0:T(8,128)(2,1)} %gather_fusion.1, pred[16]{0:T(512)(128)(4,1)S(1)} %get-tuple-element.249, bf16[96,256,128]{2,1,0:T(8,128)(2,1)} %get-tuple-element.281, s32[]{:T(128)S(6)} %select_n.101), kind=kOutput, calls=%fused_computation.5.clone.1 | convolution fusion | flops 810024960 | bytes 13631572 | tf_op jit(solution)/shard_map/while/body/pil,pik->lpk/dot_general | solution.py:39
  279.1 6.5 copy.17
  285.6 15.1 %scatter_fusion.1 = f32[768,16,128]{2,0,1:T(8,128)} fusion(f32[768,16,128]{2,0,1:T(8,128)} %get-tuple-element.265, s32[16]{0:T(128)S(1)} %get-tuple-element.247, f32[16,768,128]{2,1,0:T(8,128)} %copy.17), kind=kCustom, calls=%fused_computation.3.clone.clone.1 | custom fusion | flops 1572864 | bytes 18874432 | tf_op jit(solution)/shard_map/while/body/scatter-add | solution.py:43
  304.3 6.5 broadcast_multiply_fusion.2
  310.8 17.6 %scatter_fusion = f32[8,256,512]{2,1,0:T(8,128)} fusion(f32[8,256,512]{2,1,0:T(8,128)} %get-tuple-element.264, s32[16]{0:T(128)S(1)} %get-tuple-element.244, f32[16,256,512]{2,1,0:T(8,128)} %broadcast_multiply_fusion.2), kind=kCustom, calls=%fused_computation.2.clone.clone.1 | custom fusion | flops 2097152 | bytes 25165888 | tf_op jit(solution)/shard_map/while/body/scatter-add | solution.py:42
  332.7 7.2 %multiply_bitcast_fusion.2 = f32[16,768,128]{1,2,0:T(8,128)} fusion(f32[16]{0:T(128)S(1)} %get-tuple-element.245, bf16[16,256,768]{2,1,0:T(8,128)(2,1)} %gather_fusion.1, pred[16]{0:T(512)(128)(4,1)S(1)} %get-tuple-element.249, bf16[96,256,128]{2,1,0:T(8,128)(2,1)} %get-tuple-element.281, s32[]{:T(128)S(6)} %select_n.101), kind=kOutput, calls=%fused_computation.5.clone.1 | convolution fusion | flops 810024960 | bytes 13631572 | tf_op jit(solution)/shard_map/while/body/pil,pik->lpk/dot_general | solution.py:39
  339.9 6.5 copy.17
  346.4 15.1 %scatter_fusion.1 = f32[768,16,128]{2,0,1:T(8,128)} fusion(f32[768,16,128]{2,0,1:T(8,128)} %get-tuple-element.265, s32[16]{0:T(128)S(1)} %get-tuple-element.247, f32[16,768,128]{2,1,0:T(8,128)} %copy.17), kind=kCustom, calls=%fused_computation.3.clone.clone.1 | custom fusion | flops 1572864 | bytes 18874432 | tf_op jit(solution)/shard_map/while/body/scatter-add | solution.py:43
  365.2 6.5 broadcast_multiply_fusion.2
  371.7 18.0 %scatter_fusion = f32[8,256,512]{2,1,0:T(8,128)} fusion(f32[8,256,512]{2,1,0:T(8,128)} %get-tuple-element.264, s32[16]{0:T(128)S(1)} %get-tuple-element.244, f32[16,256,512]{2,1,0:T(8,128)} %broadcast_multiply_fusion.2), kind=kCustom, calls=%fused_computation.2.clone.clone.1 | custom fusion | flops 2097152 | bytes 25165888 | tf_op jit(solution)/shard_map/while/body/scatter-add | solution.py:42
  389.7 112.0 %reduce-scatter.4.cloned.1.call-done = f32[512,512]{1,0:T(8,128)} async-done(((f32[2048,512]{1,0:T(8,128)}), f32[512,512]{1,0:T(8,128)}) %reduce-scatter.4.cloned.1.call-update) | async-done | bytes 1048592 | tf_op jit(solution)/shard_map/reduce_scatter | solution.py:54
  501.8 29.9 %reduce-scatter.6.cloned.1.call-done = f32[128,512]{1,0:T(8,128)} async-done(((f32[512,512]{1,0:T(8,128)}), f32[128,512]{1,0:T(8,128)}) %reduce-scatter.6.cloned.1.call-update) | async-done | bytes 262160 | tf_op jit(solution)/shard_map/reduce_scatter | solution.py:55
  534.8 6.3 copy_bitcast_fusion
  541.1 126.8 %all-reduce.2.cloned.1.call-done = f32[768,512]{1,0:T(8,128)} async-done(((f32[768,512]{1,0:T(8,128)}), f32[768,512]{1,0:T(8,128)}) %all-reduce.2.cloned.1.call-update) | async-done | bytes 1572880 | tf_op jit(solution)/shard_map/psum | solution.py:64
  670.0 15.3 %reduce-scatter.8.cloned.1.call-done = f32[384,2048]{1,0:T(8,128)} async-done(((f32[768,2048]{1,0:T(8,128)}), f32[384,2048]{1,0:T(8,128)}) %reduce-scatter.8.cloned.1.call-update) | async-done | bytes 3145744 | tf_op jit(solution)/shard_map/reduce_scatter | solution.py:56
  (50 shorter events, 58.5 us)
Async XLA Ops:
  7.2 67.8 %all-gather.2.cloned.1.call-start = ((), (), s32[]{:S(2)}) async-start(), calls=%async_computation.3 | async-start | bytes 3932160 | tf_op jit(solution)/shard_map/all_gather | solution.py:17
  7.9 493.9 %reduce-scatter.4.cloned.1.call-start = ((), (), s32[]{:S(2)}) async-start(), calls=%async_computation.4 | async-start | bytes 5242880 | tf_op jit(solution)/shard_map/reduce_scatter | solution.py:54
  78.1 5.9 copy-start.1
  389.7 142.1 %reduce-scatter.6.cloned.1.call-start = ((), (), s32[]{:S(2)}) async-start(), calls=%async_computation.5 | async-start | bytes 1310720 | tf_op jit(solution)/shard_map/reduce_scatter | solution.py:55
  501.8 166.1 %all-reduce.2.cloned.1.call-start = ((), (), s32[]{:S(2)}) async-start(), calls=%async_computation.7 | async-start | bytes 3145728 | tf_op jit(solution)/shard_map/psum | solution.py:64
  534.7 150.5 %reduce-scatter.8.cloned.1.call-start = ((), (), s32[]{:S(2)}) async-start(), calls=%async_computation.6 | async-start | bytes 9437184 | tf_op jit(solution)/shard_map/reduce_scatter | solution.py:56
  541.1 144.1 %copy-start = (f32[384,2048]{1,0:T(8,128)S(1)}, f32[384,2048]{1,0:T(8,128)}, u32[]{:S(2)}) copy-start(f32[384,2048]{1,0:T(8,128)} %param.13) | copy-start | bytes 9437188
Sparse Core Ops, SparseCore 0:
  9.5 65.3 all-gather.1
  389.8 111.9 reduce-scatter.3
  504.6 27.0 reduce-scatter.5
  537.4 130.4 all-reduce.1
  670.1 15.1 reduce-scatter.7
where the time goes:
time: 697 us; the launch traced here: 696 us
  waiting for transfers between devices  351 us (50%)
  other arithmetic  173 us (25%)
  local copies, waits for them, and re-layouts  85.8 us (12%)
  matrix products  71.3 us (10%)
  between operations  14.5 us (2%)
    psum x1, waiting for transfers between devices, body(): core_total = lax.psum(core_part, ('cell', 'gene', 'rank'))  127 us
    reduce_scatter x1, waiting for transfers between devices, body(): lax.psum_scatter(right_flat, 'gene', scatter_dimension=0, tiled=True)  112 us
    scatter-add x5, other arithmetic, visit(): right_acc = right_acc.at[row_block].add(right_terms)  89.7 us
    scatter-add x5, other arithmetic, visit(): gene_acc = gene_acc.at[:, gene_block].add(gene_terms)  75.5 us
    all_gather x1, waiting for transfers between devices, body(): left_full = lax.all_gather(test_left, 'rank', axis=1, tiled=True)  66.3 us
    dot_general x5, matrix products, visit(): jnp.einsum('pil,pik->lpk', left_rows, group_tiles, preferred_element_type...  35.9 us
    mul x5, local copies, waits for them, and re-layouts, visit(): jnp.einsum('pil,pik->lpk', left_rows, group_tiles, preferred_element_type...  32.7 us
    dot_general x5, matrix products, visit(): jnp.einsum('pik,pkr->pir', group_tiles, right_rows, preferred_element_typ...  32.4 us
  transfers between devices with their start and end apart: 5, of which 5 were waited for; matrix products, arithmetic and copies ran while one was open for 1% of the time, Pallas kernels for 0%

commit v1 on v0

--- a/solution.py
+++ b/solution.py
@@ -61,7 +61,7 @@
         jnp.float32
     )
     core_part = lax.dot_general(left_mine, right_mine, (((0,), (0,)), ((), ())), precision=highest)
-    core_total = lax.psum(core_part, ("cell", "gene", "rank"))
+    core_total = lax.psum(lax.psum(core_part, ("gene", "rank")), "cell")
     share = left_width // lax.axis_size("cell")
     core = lax.dynamic_slice_in_dim(core_total, lax.axis_index("cell") * share, share, 0)
     return (right_mine, gene_sketch, core)

time: 697 us -> 705 us (1.011)
    psum x1 -> x2, waiting for transfers between devices: 127 us -> 132 us  [body(): core_total = lax.psum(lax.psum(core_part, ('gene', 'rank')), 'cell')]
  transfers between devices with their start and end apart: 5 -> 6, of which waited for: 5 -> 6; matrix products, arithmetic and copies ran while one was open for 1% -> 1% of each run, Pallas kernels for 0% -> 0%
where the time goes in v1:
time: 705 us; the launch traced here: 703 us
  waiting for transfers between devices  358 us (51%)
  other arithmetic  173 us (25%)
  local copies, waits for them, and re-layouts  85.9 us (12%)
  matrix products  71.3 us (10%)
  between operations  14.8 us (2%)
    psum x2, waiting for transfers between devices, body(): core_total = lax.psum(lax.psum(core_part, ('gene', 'rank')), 'cell')  132 us
    reduce_scatter x1, waiting for transfers between devices, body(): lax.psum_scatter(right_flat, 'gene', scatter_dimension=0, tiled=True)  112 us
    scatter-add x5, other arithmetic, visit(): right_acc = right_acc.at[row_block].add(right_terms)  89.7 us
    scatter-add x5, other arithmetic, visit(): gene_acc = gene_acc.at[:, gene_block].add(gene_terms)  75.5 us
    all_gather x1, waiting for transfers between devices, body(): left_full = lax.all_gather(test_left, 'rank', axis=1, tiled=True)  66.3 us
    dot_general x5, matrix products, visit(): jnp.einsum('pil,pik->lpk', left_rows, group_tiles, preferred_element_type...  35.9 us
    mul x5, local copies, waits for them, and re-layouts, visit(): jnp.einsum('pil,pik->lpk', left_rows, group_tiles, preferred_element_type...  32.7 us
    dot_general x5, matrix products, visit(): jnp.einsum('pik,pkr->pir', group_tiles, right_rows, preferred_element_typ...  32.4 us
  transfers between devices with their start and end apart: 6, of which 6 were waited for; matrix products, arithmetic and copies ran while one was open for 1% of the time, Pallas kernels for 0%

profile of v1, /device:TPU:1, one launch (start us, length us, event | category | flops | bytes accessed | tf_op | source)
XLA Modules:
  0.0 703.3 jit_solution(18394939870155386839)
XLA Ops:
  8.6 66.3 %all-gather.2.cloned.1.call-done = bf16[2048,768]{0,1:T(8,128)(2,1)} async-done(((bf16[2048,192]{0,1:T(8,128)(2,1)}), bf16[2048,768]{0,1:T(8,128)(2,1)}) %all-gather.2.cloned.1.call-update) | async-done | bytes 3145744 | tf_op jit(solution)/shard_map/all_gather | solution.py:17
  84.0 305.6 %while.15 = (s32[]{:T(128)}, f32[8,256,512]{2,1,0:T(8,128)}, f32[768,16,128]{2,0,1:T(8,128)}, s32[]{:T(128)}, s32[96]{0:T(128)S(1)}, /*index=5*/bf16[96,256,128]...) while((s32[]{:T(128)}, f32[8,256,512]{2,1,0:T(8,128)}, ...), condition=%wide.region_3.4_spmd.clone, body=%wide.region_0.3_spmd.clone.sunk | while | flops 1353714176 | bytes 98575488 | solution.py:51
  88.3 7.2 %multiply_bitcast_fusion.2 = f32[16,768,128]{1,2,0:T(8,128)} fusion(f32[16]{0:T(128)S(1)} %get-tuple-element.245, bf16[16,256,768]{2,1,0:T(8,128)(2,1)} %gather_fusion.1, pred[16]{0:T(512)(128)(4,1)S(1)} %get-tuple-element.249, bf16[96,256,128]{2,1,0:T(8,128)(2,1)} %get-tuple-element.281, s32[]{:T(128)S(6)} %select_n.101), kind=kOutput, calls=%fused_computation.5.clone.1 | convolution fusion | flops 810024960 | bytes 13631572 | tf_op jit(solution)/shard_map/while/body/pil,pik->lpk/dot_general | solution.py:39
  95.5 6.5 copy.17
  102.0 15.0 %scatter_fusion.1 = f32[768,16,128]{2,0,1:T(8,128)} fusion(f32[768,16,128]{2,0,1:T(8,128)} %get-tuple-element.265, s32[16]{0:T(128)S(1)} %get-tuple-element.247, f32[16,768,128]{2,1,0:T(8,128)} %copy.17), kind=kCustom, calls=%fused_computation.3.clone.clone.1 | custom fusion | flops 1572864 | bytes 18874432 | tf_op jit(solution)/shard_map/while/body/scatter-add | solution.py:43
  120.6 6.5 broadcast_multiply_fusion.2
  127.1 18.1 %scatter_fusion = f32[8,256,512]{2,1,0:T(8,128)} fusion(f32[8,256,512]{2,1,0:T(8,128)} %get-tuple-element.264, s32[16]{0:T(128)S(1)} %get-tuple-element.244, f32[16,256,512]{2,1,0:T(8,128)} %broadcast_multiply_fusion.2), kind=kCustom, calls=%fused_computation.2.clone.clone.1 | custom fusion | flops 2097152 | bytes 25165888 | tf_op jit(solution)/shard_map/while/body/scatter-add | solution.py:42
  149.4 7.2 %multiply_bitcast_fusion.2 = f32[16,768,128]{1,2,0:T(8,128)} fusion(f32[16]{0:T(128)S(1)} %get-tuple-element.245, bf16[16,256,768]{2,1,0:T(8,128)(2,1)} %gather_fusion.1, pred[16]{0:T(512)(128)(4,1)S(1)} %get-tuple-element.249, bf16[96,256,128]{2,1,0:T(8,128)(2,1)} %get-tuple-element.281, s32[]{:T(128)S(6)} %select_n.101), kind=kOutput, calls=%fused_computation.5.clone.1 | convolution fusion | flops 810024960 | bytes 13631572 | tf_op jit(solution)/shard_map/while/body/pil,pik->lpk/dot_general | solution.py:39
  156.6 6.5 copy.17
  163.2 15.3 %scatter_fusion.1 = f32[768,16,128]{2,0,1:T(8,128)} fusion(f32[768,16,128]{2,0,1:T(8,128)} %get-tuple-element.265, s32[16]{0:T(128)S(1)} %get-tuple-element.247, f32[16,768,128]{2,1,0:T(8,128)} %copy.17), kind=kCustom, calls=%fused_computation.3.clone.clone.1 | custom fusion | flops 1572864 | bytes 18874432 | tf_op jit(solution)/shard_map/while/body/scatter-add | solution.py:43
  182.1 6.5 broadcast_multiply_fusion.2
  188.5 18.0 %scatter_fusion = f32[8,256,512]{2,1,0:T(8,128)} fusion(f32[8,256,512]{2,1,0:T(8,128)} %get-tuple-element.264, s32[16]{0:T(128)S(1)} %get-tuple-element.244, f32[16,256,512]{2,1,0:T(8,128)} %broadcast_multiply_fusion.2), kind=kCustom, calls=%fused_computation.2.clone.clone.1 | custom fusion | flops 2097152 | bytes 25165888 | tf_op jit(solution)/shard_map/while/body/scatter-add | solution.py:42
  210.8 7.2 %multiply_bitcast_fusion.2 = f32[16,768,128]{1,2,0:T(8,128)} fusion(f32[16]{0:T(128)S(1)} %get-tuple-element.245, bf16[16,256,768]{2,1,0:T(8,128)(2,1)} %gather_fusion.1, pred[16]{0:T(512)(128)(4,1)S(1)} %get-tuple-element.249, bf16[96,256,128]{2,1,0:T(8,128)(2,1)} %get-tuple-element.281, s32[]{:T(128)S(6)} %select_n.101), kind=kOutput, calls=%fused_computation.5.clone.1 | convolution fusion | flops 810024960 | bytes 13631572 | tf_op jit(solution)/shard_map/while/body/pil,pik->lpk/dot_general | solution.py:39
  218.0 6.5 copy.17
  224.6 14.9 %scatter_fusion.1 = f32[768,16,128]{2,0,1:T(8,128)} fusion(f32[768,16,128]{2,0,1:T(8,128)} %get-tuple-element.265, s32[16]{0:T(128)S(1)} %get-tuple-element.247, f32[16,768,128]{2,1,0:T(8,128)} %copy.17), kind=kCustom, calls=%fused_computation.3.clone.clone.1 | custom fusion | flops 1572864 | bytes 18874432 | tf_op jit(solution)/shard_map/while/body/scatter-add | solution.py:43
  243.1 6.5 broadcast_multiply_fusion.2
  249.6 18.0 %scatter_fusion = f32[8,256,512]{2,1,0:T(8,128)} fusion(f32[8,256,512]{2,1,0:T(8,128)} %get-tuple-element.264, s32[16]{0:T(128)S(1)} %get-tuple-element.244, f32[16,256,512]{2,1,0:T(8,128)} %broadcast_multiply_fusion.2), kind=kCustom, calls=%fused_computation.2.clone.clone.1 | custom fusion | flops 2097152 | bytes 25165888 | tf_op jit(solution)/shard_map/while/body/scatter-add | solution.py:42
  271.9 7.2 %multiply_bitcast_fusion.2 = f32[16,768,128]{1,2,0:T(8,128)} fusion(f32[16]{0:T(128)S(1)} %get-tuple-element.245, bf16[16,256,768]{2,1,0:T(8,128)(2,1)} %gather_fusion.1, pred[16]{0:T(512)(128)(4,1)S(1)} %get-tuple-element.249, bf16[96,256,128]{2,1,0:T(8,128)(2,1)} %get-tuple-element.281, s32[]{:T(128)S(6)} %select_n.101), kind=kOutput, calls=%fused_computation.5.clone.1 | convolution fusion | flops 810024960 | bytes 13631572 | tf_op jit(solution)/shard_map/while/body/pil,pik->lpk/dot_general | solution.py:39
  279.1 6.5 copy.17
  285.6 15.1 %scatter_fusion.1 = f32[768,16,128]{2,0,1:T(8,128)} fusion(f32[768,16,128]{2,0,1:T(8,128)} %get-tuple-element.265, s32[16]{0:T(128)S(1)} %get-tuple-element.247, f32[16,768,128]{2,1,0:T(8,128)} %copy.17), kind=kCustom, calls=%fused_computation.3.clone.clone.1 | custom fusion | flops 1572864 | bytes 18874432 | tf_op jit(solution)/shard_map/while/body/scatter-add | solution.py:43
  304.3 6.5 broadcast_multiply_fusion.2
  310.8 17.6 %scatter_fusion = f32[8,256,512]{2,1,0:T(8,128)} fusion(f32[8,256,512]{2,1,0:T(8,128)} %get-tuple-element.264, s32[16]{0:T(128)S(1)} %get-tuple-element.244, f32[16,256,512]{2,1,0:T(8,128)} %broadcast_multiply_fusion.2), kind=kCustom, calls=%fused_computation.2.clone.clone.1 | custom fusion | flops 2097152 | bytes 25165888 | tf_op jit(solution)/shard_map/while/body/scatter-add | solution.py:42
  332.7 7.2 %multiply_bitcast_fusion.2 = f32[16,768,128]{1,2,0:T(8,128)} fusion(f32[16]{0:T(128)S(1)} %get-tuple-element.245, bf16[16,256,768]{2,1,0:T(8,128)(2,1)} %gather_fusion.1, pred[16]{0:T(512)(128)(4,1)S(1)} %get-tuple-element.249, bf16[96,256,128]{2,1,0:T(8,128)(2,1)} %get-tuple-element.281, s32[]{:T(128)S(6)} %select_n.101), kind=kOutput, calls=%fused_computation.5.clone.1 | convolution fusion | flops 810024960 | bytes 13631572 | tf_op jit(solution)/shard_map/while/body/pil,pik->lpk/dot_general | solution.py:39
  339.9 6.5 copy.17
  346.4 15.1 %scatter_fusion.1 = f32[768,16,128]{2,0,1:T(8,128)} fusion(f32[768,16,128]{2,0,1:T(8,128)} %get-tuple-element.265, s32[16]{0:T(128)S(1)} %get-tuple-element.247, f32[16,768,128]{2,1,0:T(8,128)} %copy.17), kind=kCustom, calls=%fused_computation.3.clone.clone.1 | custom fusion | flops 1572864 | bytes 18874432 | tf_op jit(solution)/shard_map/while/body/scatter-add | solution.py:43
  365.2 6.5 broadcast_multiply_fusion.2
  371.7 18.0 %scatter_fusion = f32[8,256,512]{2,1,0:T(8,128)} fusion(f32[8,256,512]{2,1,0:T(8,128)} %get-tuple-element.264, s32[16]{0:T(128)S(1)} %get-tuple-element.244, f32[16,256,512]{2,1,0:T(8,128)} %broadcast_multiply_fusion.2), kind=kCustom, calls=%fused_computation.2.clone.clone.1 | custom fusion | flops 2097152 | bytes 25165888 | tf_op jit(solution)/shard_map/while/body/scatter-add | solution.py:42
  389.7 112.0 %reduce-scatter.4.cloned.1.call-done = f32[512,512]{1,0:T(8,128)} async-done(((f32[2048,512]{1,0:T(8,128)}), f32[512,512]{1,0:T(8,128)}) %reduce-scatter.4.cloned.1.call-update) | async-done | bytes 1048592 | tf_op jit(solution)/shard_map/reduce_scatter | solution.py:54
  501.8 29.9 %reduce-scatter.6.cloned.1.call-done = f32[128,512]{1,0:T(8,128)} async-done(((f32[512,512]{1,0:T(8,128)}), f32[128,512]{1,0:T(8,128)}) %reduce-scatter.6.cloned.1.call-update) | async-done | bytes 262160 | tf_op jit(solution)/shard_map/reduce_scatter | solution.py:55
  541.2 112.0 %all-reduce.3.cloned.1.call-done = f32[768,512]{1,0:T(8,128)} async-done(((f32[768,512]{1,0:T(8,128)}), f32[768,512]{1,0:T(8,128)}) %all-reduce.3.cloned.1.call-update) | async-done | bytes 1572880 | tf_op jit(solution)/shard_map/psum | solution.py:64
  653.3 17.4 %reduce-scatter.8.cloned.1.call-done = f32[384,2048]{1,0:T(8,128)} async-done(((f32[768,2048]{1,0:T(8,128)}), f32[384,2048]{1,0:T(8,128)}) %reduce-scatter.8.cloned.1.call-update) | async-done | bytes 3145744 | tf_op jit(solution)/shard_map/reduce_scatter | solution.py:56
  674.7 19.7 %all-reduce.5.cloned.1.call-done = f32[768,512]{1,0:T(8,128)} async-done(((f32[768,512]{1,0:T(8,128)}), f32[768,512]{1,0:T(8,128)}) %all-reduce.5.cloned.1.call-update) | async-done | bytes 1572880 | tf_op jit(solution)/shard_map/psum | solution.py:64
  (53 shorter events, 64.9 us)
Async XLA Ops:
  7.2 67.8 %all-gather.2.cloned.1.call-start = ((), (), s32[]{:S(2)}) async-start(), calls=%async_computation.3 | async-start | bytes 3932160 | tf_op jit(solution)/shard_map/all_gather | solution.py:17
  7.9 493.9 %reduce-scatter.4.cloned.1.call-start = ((), (), s32[]{:S(2)}) async-start(), calls=%async_computation.4 | async-start | bytes 5242880 | tf_op jit(solution)/shard_map/reduce_scatter | solution.py:54
  78.1 5.9 copy-start.1
  389.7 142.1 %reduce-scatter.6.cloned.1.call-start = ((), (), s32[]{:S(2)}) async-start(), calls=%async_computation.5 | async-start | bytes 1310720 | tf_op jit(solution)/shard_map/reduce_scatter | solution.py:55
  501.8 151.5 %all-reduce.3.cloned.1.call-start = ((), (), s32[]{:S(2)}) async-start(), calls=%async_computation.7 | async-start | bytes 3145728 | tf_op jit(solution)/shard_map/psum | solution.py:64
  534.7 135.9 %reduce-scatter.8.cloned.1.call-start = ((), (), s32[]{:S(2)}) async-start(), calls=%async_computation.6 | async-start | bytes 9437184 | tf_op jit(solution)/shard_map/reduce_scatter | solution.py:56
  541.2 129.5 %copy-start = (f32[384,2048]{1,0:T(8,128)S(1)}, f32[384,2048]{1,0:T(8,128)}, u32[]{:S(2)}) copy-start(f32[384,2048]{1,0:T(8,128)} %param.13) | copy-start | bytes 9437188
  541.2 153.2 %all-reduce.5.cloned.1.call-start = ((), (), s32[]{:S(2)}) async-start(), calls=%async_computation.8 | async-start | bytes 3145728 | tf_op jit(solution)/shard_map/psum | solution.py:64
Sparse Core Ops, SparseCore 0:
  9.5 65.3 all-gather.1
  389.8 111.9 reduce-scatter.3
  504.6 27.0 reduce-scatter.5
  537.6 115.6 all-reduce.2
  655.4 15.1 reduce-scatter.7
  672.8 21.5 all-reduce.4
